TPU v7x, 32 devices: a whole 2x2x4 slice. The times are simulated.
32 devices in a mesh: left: 8 (over y, x, core), right: 4 (over z).
Axes of the slice: x: 2, y: 2, z: 4, core: 2. Of those that a mesh axis runs over, the one named last changes fastest.
Arguments:
- left_freq: float32 [16384], P('left'), as said below
- right_freq: float32 [16384], P('right'), as said below
- left_dirs: float32 [16, 16384], P(None, 'left'), may hold values from -6 to 6
- left_data: float32 [16, 16384], P(None, 'left'), may hold values from -6 to 6
- right_dirs: float32 [16, 16384], P(None, 'right'), may hold values from -6 to 6
- right_data: float32 [16, 16384], P(None, 'right'), may hold values from -6 to 6
- col_sketch: bfloat16 [16384, 256], P('right'), may hold values from -0.047265625 to 0.047265625
- row_sketch: bfloat16 [16384, 256], P('left'), may hold values from -0.047265625 to 0.047265625
Outputs:
- row_scaled: float32 [16384, 256], P(('left', 'right'))
- col_scaled: float32 [16384, 256], P('right')
- lower_reduced: float32 [256, 256], replicated
- shifted_reduced: float32 [256, 256], replicated
Inputs may be any that keep to these rules, and one draw needn't show every extreme that they name: left_freq[i] = 1 + (k + e) / 16384 with k distinct whole numbers of 0 to 16383 and |e| at most 0.2. right_freq[j] = 1 + (k + 0.5 + e) / 16384 with k distinct whole numbers of 0 to 16383 and |e| at most 0.2; left and right frequencies share the spacing 1 / 16384, so every left and right frequency differ by 0.1 / 16384 or more.
All inputs are finite; a program needn't handle non-finite values.
Results may differ from a plain program's by a relative error of at most 0.0089.
Values sent between devices are 32-bit elements; how exact they have to be, the bound alone decides.
A program may use at most 256 MiB of HBM per device.

v0:
```python
import math
import jax
import jax.numpy as jnp
from jax import lax
from jax.sharding import PartitionSpec as P

precise = lax.Precision.HIGHEST


def build_tiles(freq_rows, dirs_rows, data_rows, right_freq, right_dirs, right_data, total_rows):
    direct = lax.dot_general(
        data_rows,
        right_dirs,
        (((0,), (0,)), ((), ())),
        precision=precise,
        preferred_element_type=jnp.float32,
    )
    crossed = lax.dot_general(
        dirs_rows,
        right_data,
        (((0,), (0,)), ((), ())),
        precision=precise,
        preferred_element_type=jnp.float32,
    )
    spacing_gap = total_rows * (freq_rows[:, None] - right_freq[None, :])
    lower_tile = ((direct - crossed) / spacing_gap).astype(jnp.bfloat16)
    shift_tile = (
        (freq_rows[:, None] * direct - right_freq[None, :] * crossed) / spacing_gap
    ).astype(jnp.bfloat16)
    return (lower_tile, shift_tile)


def gram_of(basis):
    return lax.dot_general(
        basis,
        basis,
        (((0,), (0,)), ((), ())),
        precision=precise,
        preferred_element_type=jnp.float32,
    )


def apply_factor(basis, gram_sum, shifted_flag):
    width = gram_sum.shape[0]
    identity = jnp.eye(width, dtype=jnp.float32)
    if shifted_flag:
        gram_sum = gram_sum + 1e-05 * jnp.trace(gram_sum) / width * identity
    factor = jnp.linalg.cholesky(gram_sum)
    inverse = jax.scipy.linalg.solve_triangular(factor, identity, lower=True)
    return lax.dot_general(
        basis,
        inverse,
        (((1,), (1,)), ((), ())),
        precision=precise,
        preferred_element_type=jnp.float32,
    )


def body(
    left_freq, right_freq, left_dirs, left_data, right_dirs, right_data, col_sketch, row_sketch
):
    row_count = left_freq.shape[0]
    col_count = right_freq.shape[0]
    total_rows = row_count * lax.axis_size("left")
    total_cols = col_count * lax.axis_size("right")
    lower_tile, shift_tile = build_tiles(
        left_freq, left_dirs, left_data, right_freq, right_dirs, right_data, total_rows
    )
    row_image = lax.psum(
        jnp.dot(lower_tile, col_sketch, preferred_element_type=jnp.float32), "right"
    )
    col_image = lax.psum(
        lax.dot_general(
            lower_tile, row_sketch, (((0,), (0,)), ((), ())), preferred_element_type=jnp.float32
        ),
        "left",
    )
    row_full, col_full = (row_image, col_image)
    for sweep_index in range(2):
        gram_rows = lax.psum(gram_of(row_full), "left")
        gram_cols = lax.psum(gram_of(col_full), "right")
        row_full = apply_factor(row_full, gram_rows, sweep_index == 0)
        col_full = apply_factor(col_full, gram_cols, sweep_index == 0)
    share_rows = row_count // lax.axis_size("right")
    row_part = lax.dynamic_slice_in_dim(
        row_full, lax.axis_index("right") * share_rows, share_rows, 0
    )
    col_round = col_full.astype(jnp.bfloat16)
    lower_applied = jnp.dot(lower_tile, col_round, preferred_element_type=jnp.float32)
    shift_applied = jnp.dot(shift_tile, col_round, preferred_element_type=jnp.float32)
    lower_part = lax.dot_general(
        row_full,
        lower_applied,
        (((0,), (0,)), ((), ())),
        precision=precise,
        preferred_element_type=jnp.float32,
    )
    shift_part = lax.dot_general(
        row_full,
        shift_applied,
        (((0,), (0,)), ((), ())),
        precision=precise,
        preferred_element_type=jnp.float32,
    )
    lower_reduced, shifted_reduced = lax.psum((lower_part, shift_part), ("left", "right"))
    return (
        row_part * math.sqrt(total_rows),
        col_full * math.sqrt(total_cols),
        lower_reduced,
        shifted_reduced,
    )


def solution(mesh):
    in_specs = (
        P("left"),
        P("right"),
        P(None, "left"),
        P(None, "left"),
        P(None, "right"),
        P(None, "right"),
        P("right", None),
        P("left", None),
    )
    out_specs = (P(("left", "right"), None), P("right", None), P(), P())
    return jax.shard_map(body, mesh=mesh, in_specs=in_specs, out_specs=out_specs, check_vma=False)
```

profile of v0, /device:TPU:0, one launch (start us, length us, event | category | flops | bytes accessed | tf_op | source)
XLA Modules:
  0.0 872.8 jit_solution(7962259193701451676)
XLA Ops:
  7.3 31.2 %fusion.62 = f32[2048,4096]{1,0:T(8,128)} fusion(f32[16,2048]{1,0:T(8,128)} %param.13, f32[16,4096]{1,0:T(8,128)} %param.16), kind=kOutput, calls=%fused_computation.136 | convolution fusion | flops 1610612736 | bytes 33947648 | tf_op jit(solution)/shard_map/dot_general | solution.py:18
  38.5 40.1 %divide_convert_fusion.1 = (bf16[2048,4096]{1,0:T(8,128)(2,1)}, f32[2048,4096]{1,0:T(8,128)}) fusion(f32[2048,4096]{1,0:T(8,128)} %fusion.62, f32[4096]{0:T(1024)S(1)} %copy-done.8, f32[2048]{0:T(1024)S(1)} %copy-done.9, f32[16,2048]{1,0:T(8,128)S(1)} %copy-done.7, f32[16,4096]{1,0:T(8,128)S(1)} %copy-done.6), kind=kOutput, calls=%fused_computation.9 | convolution fusion | flops 1652555776 | bytes 84303872 | tf_op jit(solution)/shard_map/dot_general | solution.py:11
  88.3 10.5 %fusion.66 = f32[4096,256]{1,0:T(8,128)} fusion(bf16[2048,4096]{1,0:T(8,128)(2,1)} %get-tuple-element.96, bf16[2048,256]{1,0:T(8,128)(2,1)S(1)} %copy-done.5), kind=kOutput, calls=%fused_computation.140 | convolution fusion | flops 4294967296 | bytes 22020096 | tf_op jit(solution)/shard_map/dot_general | solution.py:73
  98.8 78.8 %all-reduce.10.cloned.1.call-done = f32[2048,256]{1,0:T(8,128)} async-done(((f32[2048,256]{1,0:T(8,128)}), f32[2048,256]{1,0:T(8,128)}) %all-reduce.10.cloned.1.call-update) | async-done | bytes 2097168 | tf_op jit(solution)/shard_map/psum | solution.py:69
  184.3 52.3 %all-reduce.12.cloned.1.call-done = f32[256,256]{0,1:T(8,128)} async-done(((f32[256,256]{0,1:T(8,128)}), f32[256,256]{0,1:T(8,128)}) %all-reduce.12.cloned.1.call-update) | async-done | bytes 262160 | tf_op jit(solution)/shard_map/psum | solution.py:80
  241.0 11.7 %cholesky.214 = f32[128,128]{1,0:T(8,128)S(1)} custom-call(f32[128,128]{1,0:T(8,128)S(1)} %cholesky.346), custom_call_target="Cholesky" | custom-call | tf_op jit(solution)/shard_map/jit(cholesky)/cholesky | solution.py:48
  252.7 9.8 %custom-call.17 = f32[1,128,128]{1,2,0:T(8,128)S(1)} custom-call(f32[1,128,128]{2,1,0:T(8,128)S(1)} %get-tuple-element.95), custom_call_target="InvertDiagBlocksLowerTriangular" | custom-call | tf_op jit(solution)/shard_map/jit(cholesky)/cholesky | solution.py:48
  263.1 11.7 %cholesky.231 = f32[128,128]{1,0:T(8,128)S(1)} custom-call(f32[128,128]{1,0:T(8,128)S(1)} %convolution_subtract_fusion.7), custom_call_target="Cholesky" | custom-call | tf_op jit(solution)/shard_map/jit(cholesky)/cholesky | solution.py:48
  281.1 19.7 %custom-call.18 = f32[2,128,128]{1,2,0:T(8,128)S(1)} custom-call(f32[2,128,128]{2,1,0:T(8,128)S(1)} %get-tuple-element.32), custom_call_target="InvertDiagBlocksLowerTriangular" | custom-call | tf_op jit(solution)/shard_map/jit(_solve_triangular)/triangular_solve | solution.py:49
  310.0 83.1 %all-reduce.20.cloned.1.call-done = (f32[256,256]{0,1:T(8,128)}, f32[4096,256]{1,0:T(8,128)}) async-done(((f32[256,256]{0,1:T(8,128)}, f32[4096,256]{1,0:T(8,128)}), (f32[256,256]{0,1:T(8,128)}, f32[4096,256]{1,0:T(8,128)})) %all-reduce.20.cloned.1.call-update) | async-done | bytes 4456464 | tf_op jit(solution)/shard_map/psum | solution.py:80
  395.2 11.7 %cholesky.248 = f32[128,128]{1,0:T(8,128)S(1)} custom-call(f32[128,128]{1,0:T(8,128)S(1)} %cholesky.349), custom_call_target="Cholesky" | custom-call | tf_op jit(solution)/shard_map/jit(cholesky)/cholesky | solution.py:48
  417.9 11.7 %cholesky.265 = f32[128,128]{1,0:T(8,128)S(1)} custom-call(f32[128,128]{1,0:T(8,128)S(1)} %convolution_subtract_fusion.6), custom_call_target="Cholesky" | custom-call | tf_op jit(solution)/shard_map/jit(cholesky)/cholesky | solution.py:48
  435.9 19.7 %custom-call.20 = f32[2,128,128]{1,2,0:T(8,128)S(1)} custom-call(f32[2,128,128]{2,1,0:T(8,128)S(1)} %get-tuple-element.33), custom_call_target="InvertDiagBlocksLowerTriangular" | custom-call | tf_op jit(solution)/shard_map/jit(_solve_triangular)/triangular_solve | solution.py:49
  455.9 10.9 %fusion.67 = f32[256,256]{0,1:T(8,128)} fusion(f32[4096,256]{1,0:T(8,128)} %get-tuple-element.71), kind=kOutput, calls=%fused_computation.141 | convolution fusion | flops 3221225472 | bytes 4456448 | tf_op jit(solution)/shard_map/dot_general | solution.py:34
  467.8 34.5 %all-reduce.14.cloned.1.call-done = f32[256,256]{0,1:T(8,128)} async-done(((f32[256,256]{0,1:T(8,128)}), f32[256,256]{0,1:T(8,128)}) %all-reduce.14.cloned.1.call-update) | async-done | bytes 262160 | tf_op jit(solution)/shard_map/psum | solution.py:81
  506.7 11.7 %cholesky.282 = f32[128,128]{1,0:T(8,128)S(1)} custom-call(f32[128,128]{1,0:T(8,128)S(1)} %cholesky.352), custom_call_target="Cholesky" | custom-call | tf_op jit(solution)/shard_map/jit(cholesky)/cholesky | solution.py:48
  529.4 11.7 %cholesky.299 = f32[128,128]{1,0:T(8,128)S(1)} custom-call(f32[128,128]{1,0:T(8,128)S(1)} %convolution_subtract_fusion.5), custom_call_target="Cholesky" | custom-call | tf_op jit(solution)/shard_map/jit(cholesky)/cholesky | solution.py:48
  547.5 19.7 %custom-call.22 = f32[2,128,128]{1,2,0:T(8,128)S(1)} custom-call(f32[2,128,128]{2,1,0:T(8,128)S(1)} %get-tuple-element.34), custom_call_target="InvertDiagBlocksLowerTriangular" | custom-call | tf_op jit(solution)/shard_map/jit(_solve_triangular)/triangular_solve | solution.py:49
  586.4 31.8 %all-reduce.16.cloned.1.call-done = f32[256,256]{0,1:T(8,128)} async-done(((f32[256,256]{0,1:T(8,128)}), f32[256,256]{0,1:T(8,128)}) %all-reduce.16.cloned.1.call-update) | async-done | bytes 262160 | tf_op jit(solution)/shard_map/psum | solution.py:81
  620.3 11.7 %cholesky.316 = f32[128,128]{1,0:T(8,128)S(1)} custom-call(f32[128,128]{1,0:T(8,128)S(1)} %cholesky.355), custom_call_target="Cholesky" | custom-call | tf_op jit(solution)/shard_map/jit(cholesky)/cholesky | solution.py:48
  643.0 11.9 %cholesky.333 = f32[128,128]{1,0:T(8,128)S(1)} custom-call(f32[128,128]{1,0:T(8,128)S(1)} %convolution_subtract_fusion.4), custom_call_target="Cholesky" | custom-call | tf_op jit(solution)/shard_map/jit(cholesky)/cholesky | solution.py:48
  660.9 19.7 %custom-call.24 = f32[2,128,128]{1,2,0:T(8,128)S(1)} custom-call(f32[2,128,128]{2,1,0:T(8,128)S(1)} %get-tuple-element.35), custom_call_target="InvertDiagBlocksLowerTriangular" | custom-call | tf_op jit(solution)/shard_map/jit(_solve_triangular)/triangular_solve | solution.py:49
  698.8 24.5 %fusion = f32[2048,256]{1,0:T(8,128)} fusion(f32[2048,4096]{1,0:T(8,128)} %fusion.62, f32[2048,4096]{1,0:T(8,128)} %get-tuple-element.97, f32[4096]{0:T(1024)S(1)} %copy-done.8, f32[2048]{0:T(1024)S(1)} %copy-done.9, bf16[4096,256]{1,0:T(8,128)(2,1)S(1)} %get-tuple-element.107), kind=kOutput, calls=%fused_computation.11 | convolution fusion | flops 4353687552 | bytes 71327744 | tf_op jit(solution)/shard_map/dot_general | solution.py:90
  736.1 126.1 %all-reduce.18.cloned.1.call-done = (f32[256,256]{1,0:T(8,128)}, f32[256,256]{1,0:T(8,128)}) async-done(((f32[256,256]{1,0:T(8,128)}, f32[256,256]{1,0:T(8,128)}), (f32[256,256]{1,0:T(8,128)}, f32[256,256]{1,0:T(8,128)})) %all-reduce.18.cloned.1.call-update) | async-done | bytes 524304 | tf_op jit(solution)/shard_map/psum | solution.py:105
  (143 shorter events, 160.6 us)
Async XLA Ops:
  7.2 71.5 %copy-start = (bf16[4096,256]{1,0:T(8,128)(2,1)S(1)}, bf16[4096,256]{1,0:T(8,128)(2,1)}, u32[]{:S(2)}) copy-start(bf16[4096,256]{1,0:T(8,128)(2,1)} %param.17) | copy-start | bytes 6291460
  7.2 31.3 %copy-start.8 = (f32[4096]{0:T(1024)S(1)}, f32[4096]{0:T(1024)}, u32[]{:S(2)}) copy-start(f32[4096]{0:T(1024)} %param.12) | copy-start | bytes 49156
  7.2 31.3 %copy-start.9 = (f32[2048]{0:T(1024)S(1)}, f32[2048]{0:T(1024)}, u32[]{:S(2)}) copy-start(f32[2048]{0:T(1024)} %param.11) | copy-start | bytes 24580
  7.2 31.3 %copy-start.6 = (f32[16,4096]{1,0:T(8,128)S(1)}, f32[16,4096]{1,0:T(8,128)}, u32[]{:S(2)}) copy-start(f32[16,4096]{1,0:T(8,128)} %param.15) | copy-start | bytes 786436
  7.2 31.3 %copy-start.7 = (f32[16,2048]{1,0:T(8,128)S(1)}, f32[16,2048]{1,0:T(8,128)}, u32[]{:S(2)}) copy-start(f32[16,2048]{1,0:T(8,128)} %param.14) | copy-start | bytes 393220
  7.2 170.4 %all-reduce.10.cloned.1.call-start = ((), (), s32[]{:S(2)}) async-start(), calls=%async_computation | async-start | bytes 4194304 | tf_op jit(solution)/shard_map/psum | solution.py:69
  78.6 9.6 %copy-start.5 = (bf16[2048,256]{1,0:T(8,128)(2,1)S(1)}, bf16[2048,256]{1,0:T(8,128)(2,1)}, u32[]{:S(2)}) copy-start(bf16[2048,256]{1,0:T(8,128)(2,1)} %param.18) | copy-start | bytes 3145732
  88.2 148.4 %all-reduce.12.cloned.1.call-start = ((), (), s32[]{:S(2)}) async-start(), calls=%async_computation.1 | async-start | bytes 524288 | tf_op jit(solution)/shard_map/psum | solution.py:80
  184.0 209.1 %all-reduce.20.cloned.1.call-start = ((), (), s32[]{:S(2)}) async-start(), calls=%async_computation.5 | async-start | bytes 8912896 | tf_op jit(solution)/shard_map/psum | solution.py:80
  309.5 192.8 %all-reduce.14.cloned.1.call-start = ((), (), s32[]{:S(2)}) async-start(), calls=%async_computation.2 | async-start | bytes 524288 | tf_op jit(solution)/shard_map/psum | solution.py:81
  466.8 151.4 %all-reduce.16.cloned.1.call-start = ((), (), s32[]{:S(2)}) async-start(), calls=%async_computation.3 | async-start | bytes 524288 | tf_op jit(solution)/shard_map/psum | solution.py:81
  573.6 2.0 copy-start.2
  583.0 279.2 %all-reduce.18.cloned.1.call-start = ((), (), s32[]{:S(2)}) async-start(), calls=%async_computation.4 | async-start | bytes 1048576 | tf_op jit(solution)/shard_map/psum | solution.py:105
  723.3 6.6 copy-start.3
  723.3 6.6 copy-start.4
  723.3 142.2 %copy-start.1 = (bf16[4096,256]{1,0:T(8,128)(2,1)S(1)}, bf16[4096,256]{1,0:T(8,128)(2,1)}, u32[]{:S(2)}) copy-start(bf16[4096,256]{1,0:T(8,128)(2,1)} %param.17) | copy-start | bytes 6291460
Sparse Core Ops, SparseCore 0:
  88.3 89.1 all-reduce.9
  184.1 52.4 all-reduce.11
  309.6 83.4 all-reduce.19
  466.9 35.3 all-reduce.13
  583.1 35.0 all-reduce.15
  734.3 127.8 all-reduce.17
where the time goes:
time: 879 us; the launch traced here: 873 us
  waiting for transfers between devices  407 us (46%)
  other arithmetic  228 us (26%)
  matrix products  191 us (22%)
  local copies, waits for them, and re-layouts  23.8 us (3%)
  between operations  21.6 us (2%)
    another operation x27, other arithmetic, apply_factor(): factor = jnp.linalg.cholesky(gram_sum)  138 us
    psum x2, waiting for transfers between devices, body(): gram_rows = lax.psum(gram_of(row_full), 'left')  135 us
    psum x1, waiting for transfers between devices, body(): lax.psum((lower_part, shift_part), ('left', 'right'))  126 us
    psum x1, waiting for transfers between devices, body(): lax.psum(jnp.dot(lower_tile, col_sketch, preferred_element_type=jnp.float...  78.8 us
    another operation x9, other arithmetic, apply_factor(): inverse = jax.scipy.linalg.solve_triangular(factor, identity, lower=True)  78.8 us
    psum x2, waiting for transfers between devices, body(): gram_cols = lax.psum(gram_of(col_full), 'right')  66.4 us
    dot_general x1, matrix products, build_tiles(): lax.dot_general(data_rows, right_dirs, (((0,), (0,)), ((), ())), precisio...  40.1 us
    dot_general x1, matrix products, build_tiles(): lax.dot_general(dirs_rows, right_data, (((0,), (0,)), ((), ())), precisio...  31.2 us
  transfers between devices with their start and end apart: 6, of which 6 were waited for; matrix products, arithmetic and copies ran while one was open for 2% of the time, Pallas kernels for 0%

commit v1 on v0

--- a/solution.py
+++ b/solution.py
@@ -66,9 +66,9 @@
     lower_tile, shift_tile = build_tiles(
         left_freq, left_dirs, left_data, right_freq, right_dirs, right_data, total_rows
     )
-    row_image = lax.psum(
-        jnp.dot(lower_tile, col_sketch, preferred_element_type=jnp.float32), "right"
-    )
+    own = jnp.dot(lower_tile, col_sketch, preferred_element_type=jnp.float32)
+    shards = lax.all_gather(own, "right")
+    row_image = jnp.sum(shards, axis=0)
     col_image = lax.psum(
         lax.dot_general(
             lower_tile, row_sketch, (((0,), (0,)), ((), ())), preferred_element_type=jnp.float32

time: 879 us -> 943 us (1.073)
  waiting for transfers between devices: 407 us -> 469 us
    all_gather x0 -> x1, waiting for transfers between devices: none -> 142 us  [body(): shards = lax.all_gather(own, 'right')]
    psum x1 -> x0, waiting for transfers between devices: 78.8 us -> none  [body(): lax.psum(jnp.dot(lower_tile, col_sketch, preferred_element_type=jnp.float...]
where the time goes in v1:
time: 943 us; the launch traced here: 937 us
  waiting for transfers between devices  469 us (50%)
  other arithmetic  232 us (25%)
  matrix products  188 us (20%)
  local copies, waits for them, and re-layouts  23.8 us (3%)
  between operations  21.6 us (2%)
    all_gather x1, waiting for transfers between devices, body(): shards = lax.all_gather(own, 'right')  142 us
    another operation x27, other arithmetic, apply_factor(): factor = jnp.linalg.cholesky(gram_sum)  138 us
    psum x2, waiting for transfers between devices, body(): gram_rows = lax.psum(gram_of(row_full), 'left')  135 us
    psum x1, waiting for transfers between devices, body(): lax.psum((lower_part, shift_part), ('left', 'right'))  126 us
    another operation x9, other arithmetic, apply_factor(): inverse = jax.scipy.linalg.solve_triangular(factor, identity, lower=True)  78.8 us
    psum x2, waiting for transfers between devices, body(): gram_cols = lax.psum(gram_of(col_full), 'right')  66.4 us
    dot_general x1, matrix products, build_tiles(): lax.dot_general(data_rows, right_dirs, (((0,), (0,)), ((), ())), precisio...  40.1 us
    dot_general x1, matrix products, build_tiles(): lax.dot_general(dirs_rows, right_data, (((0,), (0,)), ((), ())), precisio...  31.2 us
  transfers between devices with their start and end apart: 6, of which 6 were waited for; matrix products, arithmetic and copies ran while one was open for 2% of the time, Pallas kernels for 0%

profile of v1, /device:TPU:0, one launch (start us, length us, event | category | flops | bytes accessed | tf_op | source)
XLA Modules:
  0.0 937.3 jit_solution(9835891311464156900)
XLA Ops:
  7.3 31.2 %fusion.62 = f32[2048,4096]{1,0:T(8,128)} fusion(f32[16,2048]{1,0:T(8,128)} %param.13, f32[16,4096]{1,0:T(8,128)} %param.16), kind=kOutput, calls=%fused_computation.136 | convolution fusion | flops 1610612736 | bytes 33947648 | tf_op jit(solution)/shard_map/dot_general | solution.py:18
  38.5 40.1 %divide_convert_fusion.1 = (bf16[2048,4096]{1,0:T(8,128)(2,1)}, f32[2048,4096]{1,0:T(8,128)}) fusion(f32[2048,4096]{1,0:T(8,128)} %fusion.62, f32[4096]{0:T(1024)S(1)} %copy-done.9, f32[2048]{0:T(1024)S(1)} %copy-done.10, f32[16,2048]{1,0:T(8,128)S(1)} %copy-done.8, f32[16,4096]{1,0:T(8,128)S(1)} %copy-done.7), kind=kOutput, calls=%fused_computation.9 | convolution fusion | flops 1652555776 | bytes 84303872 | tf_op jit(solution)/shard_map/dot_general | solution.py:11
  88.3 10.5 %fusion.66 = f32[4096,256]{1,0:T(8,128)} fusion(bf16[2048,4096]{1,0:T(8,128)(2,1)} %get-tuple-element.96, bf16[2048,256]{1,0:T(8,128)(2,1)S(1)} %copy-done.6), kind=kOutput, calls=%fused_computation.140 | convolution fusion | flops 4294967296 | bytes 22020096 | tf_op jit(solution)/shard_map/dot_general | solution.py:73
  98.8 142.0 %all-gather.3.cloned.1.call-done = f32[8192,256]{1,0:T(8,128)} async-done(((f32[2048,256]{1,0:T(8,128)}), f32[8192,256]{1,0:T(8,128)}) %all-gather.3.cloned.1.call-update) | async-done | bytes 8388624 | tf_op jit(solution)/shard_map/all_gather | solution.py:70
  249.4 51.6 %all-reduce.9.cloned.1.call-done = f32[256,256]{0,1:T(8,128)} async-done(((f32[256,256]{0,1:T(8,128)}), f32[256,256]{0,1:T(8,128)}) %all-reduce.9.cloned.1.call-update) | async-done | bytes 262160 | tf_op jit(solution)/shard_map/psum | solution.py:80
  305.4 11.7 %cholesky.214 = f32[128,128]{1,0:T(8,128)S(1)} custom-call(f32[128,128]{1,0:T(8,128)S(1)} %cholesky.346), custom_call_target="Cholesky" | custom-call | tf_op jit(solution)/shard_map/jit(cholesky)/cholesky | solution.py:48
  317.2 9.8 %custom-call.17 = f32[1,128,128]{1,2,0:T(8,128)S(1)} custom-call(f32[1,128,128]{2,1,0:T(8,128)S(1)} %get-tuple-element.95), custom_call_target="InvertDiagBlocksLowerTriangular" | custom-call | tf_op jit(solution)/shard_map/jit(cholesky)/cholesky | solution.py:48
  327.5 11.7 %cholesky.231 = f32[128,128]{1,0:T(8,128)S(1)} custom-call(f32[128,128]{1,0:T(8,128)S(1)} %convolution_subtract_fusion.7), custom_call_target="Cholesky" | custom-call | tf_op jit(solution)/shard_map/jit(cholesky)/cholesky | solution.py:48
  345.6 19.7 %custom-call.18 = f32[2,128,128]{1,2,0:T(8,128)S(1)} custom-call(f32[2,128,128]{2,1,0:T(8,128)S(1)} %get-tuple-element.32), custom_call_target="InvertDiagBlocksLowerTriangular" | custom-call | tf_op jit(solution)/shard_map/jit(_solve_triangular)/triangular_solve | solution.py:49
  374.4 83.1 %all-reduce.17.cloned.1.call-done = (f32[256,256]{0,1:T(8,128)}, f32[4096,256]{1,0:T(8,128)}) async-done(((f32[256,256]{0,1:T(8,128)}, f32[4096,256]{1,0:T(8,128)}), (f32[256,256]{0,1:T(8,128)}, f32[4096,256]{1,0:T(8,128)})) %all-reduce.17.cloned.1.call-update) | async-done | bytes 4456464 | tf_op jit(solution)/shard_map/psum | solution.py:80
  459.7 11.7 %cholesky.248 = f32[128,128]{1,0:T(8,128)S(1)} custom-call(f32[128,128]{1,0:T(8,128)S(1)} %cholesky.349), custom_call_target="Cholesky" | custom-call | tf_op jit(solution)/shard_map/jit(cholesky)/cholesky | solution.py:48
  482.4 11.7 %cholesky.265 = f32[128,128]{1,0:T(8,128)S(1)} custom-call(f32[128,128]{1,0:T(8,128)S(1)} %convolution_subtract_fusion.6), custom_call_target="Cholesky" | custom-call | tf_op jit(solution)/shard_map/jit(cholesky)/cholesky | solution.py:48
  500.3 19.7 %custom-call.20 = f32[2,128,128]{1,2,0:T(8,128)S(1)} custom-call(f32[2,128,128]{2,1,0:T(8,128)S(1)} %get-tuple-element.33), custom_call_target="InvertDiagBlocksLowerTriangular" | custom-call | tf_op jit(solution)/shard_map/jit(_solve_triangular)/triangular_solve | solution.py:49
  520.3 10.9 %fusion.67 = f32[256,256]{0,1:T(8,128)} fusion(f32[4096,256]{1,0:T(8,128)} %get-tuple-element.71), kind=kOutput, calls=%fused_computation.141 | convolution fusion | flops 3221225472 | bytes 4456448 | tf_op jit(solution)/shard_map/dot_general | solution.py:34
  532.2 34.6 %all-reduce.11.cloned.1.call-done = f32[256,256]{0,1:T(8,128)} async-done(((f32[256,256]{0,1:T(8,128)}), f32[256,256]{0,1:T(8,128)}) %all-reduce.11.cloned.1.call-update) | async-done | bytes 262160 | tf_op jit(solution)/shard_map/psum | solution.py:81
  571.1 11.7 %cholesky.282 = f32[128,128]{1,0:T(8,128)S(1)} custom-call(f32[128,128]{1,0:T(8,128)S(1)} %cholesky.352), custom_call_target="Cholesky" | custom-call | tf_op jit(solution)/shard_map/jit(cholesky)/cholesky | solution.py:48
  593.8 11.7 %cholesky.299 = f32[128,128]{1,0:T(8,128)S(1)} custom-call(f32[128,128]{1,0:T(8,128)S(1)} %convolution_subtract_fusion.5), custom_call_target="Cholesky" | custom-call | tf_op jit(solution)/shard_map/jit(cholesky)/cholesky | solution.py:48
  612.0 19.7 %custom-call.22 = f32[2,128,128]{1,2,0:T(8,128)S(1)} custom-call(f32[2,128,128]{2,1,0:T(8,128)S(1)} %get-tuple-element.34), custom_call_target="InvertDiagBlocksLowerTriangular" | custom-call | tf_op jit(solution)/shard_map/jit(_solve_triangular)/triangular_solve | solution.py:49
  650.8 31.8 %all-reduce.13.cloned.1.call-done = f32[256,256]{0,1:T(8,128)} async-done(((f32[256,256]{0,1:T(8,128)}), f32[256,256]{0,1:T(8,128)}) %all-reduce.13.cloned.1.call-update) | async-done | bytes 262160 | tf_op jit(solution)/shard_map/psum | solution.py:81
  684.8 11.7 %cholesky.316 = f32[128,128]{1,0:T(8,128)S(1)} custom-call(f32[128,128]{1,0:T(8,128)S(1)} %cholesky.355), custom_call_target="Cholesky" | custom-call | tf_op jit(solution)/shard_map/jit(cholesky)/cholesky | solution.py:48
  707.5 11.9 %cholesky.333 = f32[128,128]{1,0:T(8,128)S(1)} custom-call(f32[128,128]{1,0:T(8,128)S(1)} %convolution_subtract_fusion.4), custom_call_target="Cholesky" | custom-call | tf_op jit(solution)/shard_map/jit(cholesky)/cholesky | solution.py:48
  725.4 19.7 %custom-call.24 = f32[2,128,128]{1,2,0:T(8,128)S(1)} custom-call(f32[2,128,128]{2,1,0:T(8,128)S(1)} %get-tuple-element.35), custom_call_target="InvertDiagBlocksLowerTriangular" | custom-call | tf_op jit(solution)/shard_map/jit(_solve_triangular)/triangular_solve | solution.py:49
  763.3 24.5 %fusion = f32[2048,256]{1,0:T(8,128)} fusion(f32[2048,4096]{1,0:T(8,128)} %fusion.62, f32[2048,4096]{1,0:T(8,128)} %get-tuple-element.97, f32[4096]{0:T(1024)S(1)} %copy-done.9, f32[2048]{0:T(1024)S(1)} %copy-done.10, bf16[4096,256]{1,0:T(8,128)(2,1)S(1)} %get-tuple-element.107), kind=kOutput, calls=%fused_computation.11 | convolution fusion | flops 4353687552 | bytes 71327744 | tf_op jit(solution)/shard_map/dot_general | solution.py:90
  800.5 126.1 %all-reduce.15.cloned.1.call-done = (f32[256,256]{1,0:T(8,128)}, f32[256,256]{1,0:T(8,128)}) async-done(((f32[256,256]{1,0:T(8,128)}, f32[256,256]{1,0:T(8,128)}), (f32[256,256]{1,0:T(8,128)}, f32[256,256]{1,0:T(8,128)})) %all-reduce.15.cloned.1.call-update) | async-done | bytes 524304 | tf_op jit(solution)/shard_map/psum | solution.py:105
  (146 shorter events, 162.6 us)
Async XLA Ops:
  7.2 71.5 %copy-start = (bf16[4096,256]{1,0:T(8,128)(2,1)S(1)}, bf16[4096,256]{1,0:T(8,128)(2,1)}, u32[]{:S(2)}) copy-start(bf16[4096,256]{1,0:T(8,128)(2,1)} %param.17) | copy-start | bytes 6291460
  7.2 31.3 %copy-start.9 = (f32[4096]{0:T(1024)S(1)}, f32[4096]{0:T(1024)}, u32[]{:S(2)}) copy-start(f32[4096]{0:T(1024)} %param.12) | copy-start | bytes 49156
  7.2 31.3 %copy-start.10 = (f32[2048]{0:T(1024)S(1)}, f32[2048]{0:T(1024)}, u32[]{:S(2)}) copy-start(f32[2048]{0:T(1024)} %param.11) | copy-start | bytes 24580
  7.2 31.3 %copy-start.7 = (f32[16,4096]{1,0:T(8,128)S(1)}, f32[16,4096]{1,0:T(8,128)}, u32[]{:S(2)}) copy-start(f32[16,4096]{1,0:T(8,128)} %param.15) | copy-start | bytes 786436
  7.2 31.3 %copy-start.8 = (f32[16,2048]{1,0:T(8,128)S(1)}, f32[16,2048]{1,0:T(8,128)}, u32[]{:S(2)}) copy-start(f32[16,2048]{1,0:T(8,128)} %param.14) | copy-start | bytes 393220
  7.2 233.5 %all-gather.3.cloned.1.call-start = ((), (), s32[]{:S(2)}) async-start(), calls=%async_computation.3 | async-start | bytes 10485760 | tf_op jit(solution)/shard_map/all_gather | solution.py:70
  78.6 9.6 %copy-start.6 = (bf16[2048,256]{1,0:T(8,128)(2,1)S(1)}, bf16[2048,256]{1,0:T(8,128)(2,1)}, u32[]{:S(2)}) copy-start(bf16[2048,256]{1,0:T(8,128)(2,1)} %param.18) | copy-start | bytes 3145732
  88.2 212.8 %all-reduce.9.cloned.1.call-start = ((), (), s32[]{:S(2)}) async-start(), calls=%async_computation | async-start | bytes 524288 | tf_op jit(solution)/shard_map/psum | solution.py:80
  244.9 96.3 %copy-start.3 = (f32[2048,256]{1,0:T(8,128)}, f32[2048,256]{1,0:T(8,128)S(1)}, u32[]{:S(2)}) copy-start(f32[2048,256]{1,0:T(8,128)S(1)} %reduce_sum.25) | copy-start | bytes 6291460
  249.1 208.4 %all-reduce.17.cloned.1.call-start = ((), (), s32[]{:S(2)}) async-start(), calls=%async_computation.5 | async-start | bytes 8912896 | tf_op jit(solution)/shard_map/psum | solution.py:80
  373.9 192.8 %all-reduce.11.cloned.1.call-start = ((), (), s32[]{:S(2)}) async-start(), calls=%async_computation.1 | async-start | bytes 524288 | tf_op jit(solution)/shard_map/psum | solution.py:81
  531.2 151.5 %all-reduce.13.cloned.1.call-start = ((), (), s32[]{:S(2)}) async-start(), calls=%async_computation.2 | async-start | bytes 524288 | tf_op jit(solution)/shard_map/psum | solution.py:81
  638.0 2.0 copy-start.2
  647.4 279.2 %all-reduce.15.cloned.1.call-start = ((), (), s32[]{:S(2)}) async-start(), calls=%async_computation.4 | async-start | bytes 1048576 | tf_op jit(solution)/shard_map/psum | solution.py:105
  787.7 6.6 copy-start.4
  787.8 6.6 copy-start.5
  787.8 142.2 %copy-start.1 = (bf16[4096,256]{1,0:T(8,128)(2,1)S(1)}, bf16[4096,256]{1,0:T(8,128)(2,1)}, u32[]{:S(2)}) copy-start(bf16[4096,256]{1,0:T(8,128)(2,1)} %param.17) | copy-start | bytes 6291460
Sparse Core Ops, SparseCore 0:
  88.4 152.3 all-gather.2
  249.3 51.7 all-reduce.8
  374.1 83.4 all-reduce.16
  531.3 35.3 all-reduce.10
  647.6 35.0 all-reduce.12
  798.8 127.8 all-reduce.14
